TPU v7x, 32 devices: a whole 2x2x4 slice. The times are simulated.
32 devices in a mesh: pipe: 2 (over y), ctx: 16 (over z, x, core).
Axes of the slice: x: 2, y: 2, z: 4, core: 2. Of those that a mesh axis runs over, the one named last changes fastest.
Arguments:
- saved_qkv: bfloat16 [2, 3, 2048, 2048], P('pipe', None, 'ctx'), may hold values from -6 to 6
- handed: bfloat16 [2, 2048, 2048], P('pipe', 'ctx'), may hold values from -6 to 6
- long_filter: bfloat16 [2, 128, 128], P('pipe'), may hold values from -0.5 to 0.5
- short_filter: bfloat16 [2, 3, 3, 2048], P('pipe'), may hold values from -3.5 to 3.5
- doc_lengths: int32 [16], replicated, may hold values from 1 to 512, 2048 in all
Outputs:
- grad_pre: bfloat16 [2, 3, 2048, 2048], P('pipe', None, 'ctx')
- filter_grad: float32 [2, 128, 128], P('pipe')
Inputs may be any that keep to these rules, and one draw needn't show every extreme that they name: `doc_lengths`: documents lie end to end and sum to 2048 tokens; the longest has exactly 512 tokens.
All inputs are finite; a program needn't handle non-finite values.
Results may differ from a plain program's by a relative error of at most 0.0058.
Values may be sent and summed in bfloat16 or wider, within the bound.
A program may use at most 64 MiB of HBM per device.

v0:
```python
import functools
import math

import jax
import jax.numpy as jnp
from jax import lax
from jax.experimental import pallas as pl
from jax.experimental.pallas import tpu as pltpu
from jax.sharding import PartitionSpec as P

MESH = pl.DeviceIdType.MESH
F32 = jnp.float32
BF16 = jnp.bfloat16
LANES = 128
RIM = 8


def positions(rows, docs_ref):
    latest = jnp.zeros(rows.shape, jnp.int32)
    start = jnp.int32(0)
    for doc in range(docs_ref.shape[0]):
        latest = jnp.maximum(latest, jnp.where(start <= rows, start, 0))
        start = start + docs_ref[doc]
    return rows - latest


def kernel(
    sections, devices, chunks,
    docs_ref, qkv_hbm, handed_hbm, filt_ref, short_ref,
    out_hbm, fg_ref,
    qkv, inc, zz, gg, ysc, dsc, obuf, lhs, lhs3, fdir, frev, shortf,
    m_own, m_prev, t_own, t_next, r_own, r_prev, u_rows,
    acc, part, parts_in, gath,
    in_sem, out_sem, inc_s, inc_r, z_s, z_r, g_s, g_r, rim_s, rim_r, rs_s, rs_r, ag_s, ag_r, ready,
):
    sec = lax.axis_index("pipe")
    me = lax.axis_index("ctx")
    count, channels = inc.shape
    groups = fdir.shape[0]
    members = channels // groups
    per_tile = LANES // members
    wide = channels // chunks
    tiles = wide // LANES
    share = groups // devices
    first, last = me == 0, me == devices - 1
    ahead = lax.rem(sec + sections - 1, sections)
    behind = lax.rem(sec + 1, sections)

    loads = [
        pltpu.make_async_copy(qkv_hbm.at[0, i], qkv.at[i], in_sem.at[i]) for i in range(3)
    ]
    for i in (1, 2, 0):
        loads[i].start()

    barrier = pltpu.get_barrier_semaphore()
    pl.semaphore_signal(barrier, inc=1, device_id={"pipe": behind}, device_id_type=MESH)

    for step in (1, devices - 1):
        peer = lax.rem(me + step, devices)
        pl.semaphore_signal(barrier, inc=1, device_id={"ctx": peer}, device_id_type=MESH)
    pl.semaphore_wait(barrier, 3)

    reaches = []
    while 2 ** len(reaches) < devices // 2:
        reaches.append(2 ** len(reaches))

    def tell(r):
        if r < len(reaches):
            for step in (reaches[r], devices - reaches[r]):
                peer = lax.rem(me + step, devices)
                pl.semaphore_signal(
                    ready.at[r], inc=1, device_id={"ctx": peer}, device_id_type=MESH)

    def hear(r):
        if r < len(reaches):
            pl.semaphore_wait(ready.at[r], 2)

    def cols(c):
        return pl.ds(c * wide, wide)

    def send_inc(c):
        return pltpu.make_async_remote_copy(
            handed_hbm.at[0, :, cols(c)], inc.at[:, cols(c)], inc_s.at[c], inc_r.at[c],
            device_id={"pipe": ahead}, device_id_type=MESH)

    def send_z(c):
        return pltpu.make_async_remote_copy(
            zz.at[pl.ds(0, count), cols(c)], zz.at[pl.ds(count, count), cols(c)],
            z_s.at[c], z_r.at[c],
            device_id={"ctx": lax.rem(me + 1, devices)}, device_id_type=MESH)

    def send_g(c):
        return pltpu.make_async_remote_copy(
            gg.at[pl.ds(0, count), cols(c)], gg.at[pl.ds(count, count), cols(c)],
            g_s.at[c], g_r.at[c],
            device_id={"ctx": lax.rem(me + devices - 1, devices)}, device_id_type=MESH)

    def send_rim(c):
        return pltpu.make_async_remote_copy(
            dsc.at[:, pl.ds(0, RIM), cols(c)], dsc.at[:, pl.ds(count, RIM), cols(c)],
            rim_s.at[c], rim_r.at[c],
            device_id={"ctx": lax.rem(me + devices - 1, devices)}, device_id_type=MESH)

    def send_part(k):
        peer = lax.rem(me + k, devices)
        return pltpu.make_async_remote_copy(
            part.at[peer], parts_in.at[k], rs_s.at[k], rs_r.at[k],
            device_id={"ctx": peer}, device_id_type=MESH)

    def send_sum(k):
        peer = lax.rem(me + k, devices)
        return pltpu.make_async_remote_copy(
            gath.at[me], gath.at[me], ag_s.at[k], ag_r.at[k],
            device_id={"ctx": peer}, device_id_type=MESH)

    def take_sum(k):
        peer = lax.rem(me + devices - k, devices)
        return pltpu.make_async_remote_copy(
            gath.at[peer], gath.at[peer], ag_s.at[k], ag_r.at[k],
            device_id={"ctx": lax.rem(me + k, devices)}, device_id_type=MESH)

    for c in range(chunks):
        send_inc(c).start()
    tell(0)

    loads[1].wait()
    loads[2].wait()
    for c in range(chunks):
        z = qkv[1, :, cols(c)].astype(F32) * qkv[2, :, cols(c)].astype(F32)
        zz[pl.ds(0, count), cols(c)] = z.astype(BF16)

        @pl.when(jnp.logical_not(last))
        def _():
            send_z(c).start()

    @pl.when(first)
    def _():
        zz[pl.ds(count, count), :] = jnp.zeros((count, channels), BF16)

    @pl.when(last)
    def _():
        gg[pl.ds(count, count), :] = jnp.zeros((count, channels), BF16)
        dsc[:, pl.ds(count, RIM), :] = jnp.zeros((3, RIM, channels), F32)

    square = (count, count)
    down = lax.broadcasted_iota(jnp.int32, square, 0)
    across = lax.broadcasted_iota(jnp.int32, square, 1)
    base = me * count

    def one(flag):
        return jnp.where(flag, 1.0, 0.0).astype(F32)

    pos_down = positions(base + down, docs_ref)
    lag = down - across
    m_own[...] = one((lag >= 0) & (lag <= pos_down)).astype(BF16)
    m_prev[...] = one((lag < 0) & (lag + count <= pos_down)).astype(BF16)
    turned = count - 1 - down
    pos_turned = positions(base + turned, docs_ref)
    lag = turned - across
    r_own[...] = one((lag >= 0) & (lag <= pos_turned))
    r_prev[...] = one((lag < 0) & (lag + count <= pos_turned))
    line = lax.broadcasted_iota(jnp.int32, (8, count), 1)
    pos_line = positions(base + line, docs_ref)[0:1]
    pos_ahead = positions(base + count + line, docs_ref)[0:1]
    lag = across - down
    t_own[...] = one((lag >= 0) & (lag <= pos_line)).astype(BF16)
    more = jnp.where(last, 0, 1)
    t_next[...] = one((lag < 0) & (lag + count <= pos_ahead) & (more > 0)).astype(BF16)
    for j in range(1, u_rows.shape[0] + 1):
        rows = base + down[:, :LANES] + j
        u_rows[j - 1] = one((j <= positions(rows, docs_ref)) & (rows < devices * count))
    straight = one(down == across).astype(BF16)
    lapped = one((down + across == 0) | (down + across == count)).astype(BF16)
    flip = one(down + across == count - 1)
    sides = (((0,), (0,)), ((), ()))
    filt = filt_ref[0]
    fdir[...] = lax.dot_general(filt, straight, sides, preferred_element_type=F32)
    frev[...] = lax.dot_general(filt, lapped, sides, preferred_element_type=F32)
    shortf[...] = short_ref[0].astype(F32)
    lane_group = lax.broadcasted_iota(jnp.int32, (count, LANES), 1) // members

    def toeplitz(source, tile, near, far):
        block = source[pl.ds(pl.multiple_of(tile * per_tile, per_tile), per_tile), :]
        for g in range(per_tile):
            full = jnp.broadcast_to(block[g:g + 1], square)
            ring = pltpu.roll(full, 0, 1, stride=1, stride_axis=0).astype(BF16)
            lhs[g * count:(g + 1) * count, :count] = ring * near[...]
            lhs[g * count:(g + 1) * count, count:] = ring * far[...]

    def picked(product):
        total = product[:count]
        for g in range(1, per_tile):
            total = jnp.where(lane_group == g, product[g * count:(g + 1) * count], total)
        return total

    def lanes(tile):
        return pl.ds(pl.multiple_of(tile * LANES, LANES), LANES)

    for c in range(chunks):
        @pl.when(jnp.logical_not(first))
        def _():
            send_z(c).wait_recv()

        def forward(i, carry):
            tile = c * tiles + i
            toeplitz(frev, tile, m_own, m_prev)
            product = jnp.dot(lhs[...], zz[:, lanes(tile)], preferred_element_type=F32)
            ysc[:, lanes(tile)] = picked(product)
            return carry

        lax.fori_loop(0, tiles, forward, 0)
        hear(c)
        tell(c + 1)

    loads[0].wait()
    for c in range(chunks):
        send_inc(c).wait_recv()
        wide_inc = inc[:, cols(c)].astype(F32)
        gg[pl.ds(0, count), cols(c)] = (wide_inc * qkv[0, :, cols(c)].astype(F32)).astype(BF16)

        @pl.when(jnp.logical_not(first))
        def _():
            send_g(c).start()

        dsc[0, pl.ds(0, count), cols(c)] = (wide_inc * ysc[:, cols(c)]).astype(BF16).astype(F32)

        def pairs(i, carry):
            tile = c * tiles + i
            own = gg[pl.ds(0, count), lanes(tile)]
            back = jnp.dot(flip.astype(BF16), own, preferred_element_type=F32)
            for g in range(per_tile):
                lhs3[g * count:(g + 1) * count, :] = jnp.where(
                    lane_group == g, back, 0.0).astype(BF16)
            product = lax.dot_general(
                lhs3[...], zz[:, lanes(tile)], (((1,), (1,)), ((), ())),
                preferred_element_type=F32)
            sums = []
            for g in range(per_tile):
                near = product[g * count:(g + 1) * count, :count]
                far = product[g * count:(g + 1) * count, count:]
                both = near * r_own[...] + far * r_prev[...]
                slid = pltpu.roll(both, 0, 1, stride=1, stride_axis=0)
                sums.append(jnp.sum(slid, axis=0, keepdims=True))
            acc[pl.ds(pl.multiple_of(tile * per_tile, per_tile), per_tile), :] = (
                jnp.concatenate(sums, axis=0))
            return carry

        lax.fori_loop(0, tiles, pairs, 0)

    for r in range(chunks, len(reaches)):
        hear(r)
        tell(r + 1)
    for d in range(devices):
        part[d] = acc[d * share:(d + 1) * share, :]

    def start_part(k, carry):
        send_part(k).start()
        return carry

    lax.fori_loop(1, devices, start_part, 0)

    def land_part(k, total):
        send_part(k).wait_recv()
        return total + parts_in[k]


    def start_sum(k, carry):
        send_sum(k).start()
        return carry

    for c in range(chunks):
        @pl.when(jnp.logical_not(last))
        def _():
            send_g(c).wait_recv()

        def backward(i, carry):
            tile = c * tiles + i
            toeplitz(fdir, tile, t_own, t_next)
            product = jnp.dot(lhs[...], gg[:, lanes(tile)], preferred_element_type=F32)
            mixed = picked(product)
            key = qkv[1, :, lanes(tile)].astype(F32)
            value = qkv[2, :, lanes(tile)].astype(F32)
            dsc[1, pl.ds(0, count), lanes(tile)] = (mixed * value).astype(BF16).astype(F32)
            dsc[2, pl.ds(0, count), lanes(tile)] = (mixed * key).astype(BF16).astype(F32)
            return carry

        lax.fori_loop(0, tiles, backward, 0)

        @pl.when(jnp.logical_not(first))
        def _():
            send_rim(c).start()

        if c == max(chunks - 2, 0):
            gath[me] = lax.fori_loop(1, devices, land_part, part[me])
            lax.fori_loop(1, devices, start_sum, 0)

    def store(c):
        return pltpu.make_async_copy(
            obuf.at[:, :, cols(c)], out_hbm.at[0, :, :, cols(c)], out_sem.at[c])

    for c in range(chunks):
        @pl.when(jnp.logical_not(last))
        def _():
            send_rim(c).wait_recv()

        def short(i, carry):
            tile = c * tiles + i
            for s in range(3):
                total = dsc[s, pl.ds(0, count), lanes(tile)] * shortf[s, pl.ds(0, 1), lanes(tile)]
                for j in range(1, u_rows.shape[0] + 1):
                    moved = dsc[s, pl.ds(j, count), lanes(tile)]
                    weight = shortf[s, pl.ds(j, 1), lanes(tile)]
                    total = total + (moved * weight) * u_rows[j - 1]
                obuf[s, :, lanes(tile)] = total.astype(BF16)
            return carry

        lax.fori_loop(0, tiles, short, 0)
        store(c).start()

    def land_sum(k, carry):
        take_sum(k).wait_recv()
        return carry

    lax.fori_loop(1, devices, land_sum, 0)
    for d in range(devices):
        acc[d * share:(d + 1) * share, :] = gath[d]
    summed = lax.dot_general(
        flip, acc[...], (((1,), (1,)), ((), ())),
        preferred_element_type=F32, precision=lax.Precision.HIGHEST)
    fg_ref[0] = summed / math.sqrt(count * devices * members)

    def left(k, carry):
        send_part(k).wait_send()
        send_sum(k).wait_send()
        return carry

    lax.fori_loop(1, devices, left, 0)
    for c in range(chunks):
        send_inc(c).wait_send()
        store(c).wait()

        @pl.when(jnp.logical_not(last))
        def _():
            send_z(c).wait_send()

        @pl.when(jnp.logical_not(first))
        def _():
            send_g(c).wait_send()
            send_rim(c).wait_send()


def body(sections, devices, saved_qkv, handed, long_filter, short_filter, doc_lengths):
    _, _, count, channels = saved_qkv.shape
    _, taps, groups = long_filter.shape
    short_taps = short_filter.shape[2]
    assert taps == count and groups % devices == 0
    chunks = max(1, math.gcd(channels // LANES, 4))
    per_tile = LANES // (channels // groups)
    share = groups // devices
    dma = pltpu.SemaphoreType.DMA
    vmem = pltpu.VMEM
    hbm = pl.BlockSpec(memory_space=pl.ANY)
    local = pl.BlockSpec(memory_space=pltpu.VMEM)
    return pl.pallas_call(
        functools.partial(kernel, sections, devices, chunks),
        out_shape=(
            jax.ShapeDtypeStruct(saved_qkv.shape, BF16),
            jax.ShapeDtypeStruct(long_filter.shape, F32),
        ),
        in_specs=[pl.BlockSpec(memory_space=pltpu.SMEM), hbm, hbm, local, local],
        out_specs=(hbm, local),
        scratch_shapes=[
            vmem((3, count, channels), BF16),
            vmem((count, channels), BF16),
            vmem((2 * count, channels), BF16),
            vmem((2 * count, channels), BF16),
            vmem((count, channels), F32),
            vmem((3, count + RIM, channels), F32),
            vmem((3, count, channels), BF16),
            vmem((per_tile * count, 2 * count), BF16),
            vmem((per_tile * count, LANES), BF16),
            vmem((groups, count), F32),
            vmem((groups, count), F32),
            vmem((3, short_taps, channels), F32),
            vmem((count, count), BF16),
            vmem((count, count), BF16),
            vmem((count, count), BF16),
            vmem((count, count), BF16),
            vmem((count, count), F32),
            vmem((count, count), F32),
            vmem((short_taps - 1, count, LANES), F32),
            vmem((groups, count), F32),
            vmem((devices, share, count), F32),
            vmem((devices, share, count), F32),
            vmem((devices, share, count), F32),
            dma((3,)), dma((chunks,)),
            dma((chunks,)), dma((chunks,)),
            dma((chunks,)), dma((chunks,)),
            dma((chunks,)), dma((chunks,)),
            dma((chunks,)), dma((chunks,)),
            dma((devices,)), dma((devices,)),
            dma((devices,)), dma((devices,)),
            pltpu.SemaphoreType.REGULAR((max(1, devices.bit_length()),)),
        ],
        compiler_params=pltpu.CompilerParams(collective_id=0, has_side_effects=True),
    )(doc_lengths, saved_qkv, handed, long_filter, short_filter)


def solution(mesh):
    return jax.shard_map(
        functools.partial(body, mesh.shape["pipe"], mesh.shape["ctx"]),
        mesh=mesh,
        in_specs=(
            P("pipe", None, "ctx", None),
            P("pipe", "ctx", None),
            P("pipe", None, None),
            P("pipe", None, None, None),
            P(),
        ),
        out_specs=(P("pipe", None, "ctx", None), P("pipe", None, None)),
        check_vma=False,
    )
```

profile of v0, /device:TPU:0, one launch (start us, length us, event | category | flops | bytes accessed | tf_op | source)
XLA Modules:
  0.0 40.0 jit_solution(8700051101901743990)
XLA Ops:
  0.6 35.9 %shard_map.68 = (bf16[1,3,128,2048]{3,2,1,0:T(8,128)(2,1)}, f32[1,128,128]{2,1,0:T(8,128)}) custom-call(s32[16]{0:T(128)} %docs_ref.1, bf16[1,3,128,2048]{3,2,1,0:T(8,128)(2,1)} %qkv_hbm.1, bf16[1,128,2048]{2,1,0:T(8,128)(2,1)} %handed_hbm.1, bf16[1,128,128]{2,1,0:T(8,128)(2,1)} %filt_ref.1, bf16[1,3,3,2048]{3,2,1,0:T(4,128)(2,1)} %short_ref.1), custom_call_target="tpu_custom_call" | custom-call | tf_op jit(solution)/shard_map/pallas_call | solution.py:364
  36.6 0.0 copy-start
  36.6 2.8 %copy.9 = bf16[1,3,128,2048]{3,2,1,0:T(8,128)(2,1)} copy(bf16[1,3,128,2048]{3,2,1,0:T(8,128)(2,1)} %get-tuple-element.4) | data formatting | bytes 3145728
  39.3 0.0 copy-done
  39.3 0.6 %copy.10 = f32[1,128,128]{2,1,0:T(8,128)} copy(f32[1,128,128]{2,1,0:T(8,128)S(1)} %copy-done) | data formatting | bytes 131072
Async XLA Ops:
  36.6 2.8 %copy-start = (f32[1,128,128]{2,1,0:T(8,128)S(1)}, f32[1,128,128]{2,1,0:T(8,128)}, u32[]{:S(2)}) copy-start(f32[1,128,128]{2,1,0:T(8,128)} %get-tuple-element.5) | copy-start | bytes 196612
where the time goes:
time: 40.5 us; the launch traced here: 40 us
  Pallas kernels  35.9 us (89%)
  local copies, waits for them, and re-layouts  3.39 us (8%)
  between operations  0.65 us (2%)
    pallas_call x1, Pallas kernels, body(): pl.pallas_call(functools.partial(kernel, sections, devices, chunks), out_...  35.9 us
    unnamed x4, local copies, waits for them, and re-layouts  3.39 us

commit v1 on v0

v1 whole, which is shorter than its diff:
```python
import functools
import math

import jax
import jax.numpy as jnp
from jax import lax
from jax.experimental import pallas as pl
from jax.experimental.pallas import tpu as pltpu
from jax.sharding import PartitionSpec as P

MESH = pl.DeviceIdType.MESH
F32 = jnp.float32
BF16 = jnp.bfloat16
LANES = 128
RIM = 8
STRIP = 16


def positions(rows, docs_ref):
    latest = jnp.zeros(rows.shape, jnp.int32)
    start = jnp.int32(0)
    for doc in range(docs_ref.shape[0]):
        latest = jnp.maximum(latest, jnp.where(start <= rows, start, 0))
        start = start + docs_ref[doc]
    return rows - latest


def kernel(
    sections, devices, chunks, owners,
    docs_ref, qkv_hbm, handed_hbm, filt_hbm, short_hbm,
    out_hbm, sum_hbm,
    qkv, inc, zz, gg, gback, ysc, dsc, obuf, lhs_f, lhs_b, lhs_p, fdir, frev, filt, short_in, shortf,
    m_own, m_prev, t_own, t_next, r_own, r_prev, u_rows, lane_mask,
    acc, part, parts_in, gath, fg,
    in_sem, par_sem, out_sem, sum_sem, inc_s, inc_r, z_s, z_r, g_s, g_r, rim_s, rim_r, rs_s, rs_r, ag_s, ag_r,
    ready,
):
    sec = lax.axis_index("pipe")
    me = lax.axis_index("ctx")
    count, channels = inc.shape
    groups = fdir.shape[0]
    members = channels // groups
    per_tile = LANES // members
    wide = channels // chunks
    tiles = wide // LANES
    share = groups // owners
    low = (devices - owners) // 2
    first, last = me == 0, me == devices - 1
    ahead = lax.rem(sec + sections - 1, sections)
    behind = lax.rem(sec + 1, sections)
    before, after = jnp.logical_not(first), jnp.logical_not(last)

    barrier = pltpu.get_barrier_semaphore()
    pl.semaphore_signal(barrier, inc=1, device_id={"pipe": behind}, device_id_type=MESH)

    @pl.when(before)
    def _():
        pl.semaphore_signal(barrier, inc=1, device_id={"ctx": me - 1}, device_id_type=MESH)

    @pl.when(after)
    def _():
        pl.semaphore_signal(barrier, inc=1, device_id={"ctx": me + 1}, device_id_type=MESH)

    loads = [
        pltpu.make_async_copy(qkv_hbm.at[0, i], qkv.at[i], in_sem.at[i]) for i in range(3)
    ]
    for i in (1, 2, 0):
        loads[i].start()
    params = [
        pltpu.make_async_copy(filt_hbm.at[0], filt, par_sem.at[0]),
        pltpu.make_async_copy(short_hbm.at[0], short_in, par_sem.at[1]),
    ]
    for copy in params:
        copy.start()

    pl.semaphore_wait(barrier, 1 + before.astype(jnp.int32) + after.astype(jnp.int32))

    reaches = []
    while 2 ** len(reaches) < devices:
        reaches.append(2 ** len(reaches))

    def tell(r):
        if r < len(reaches):
            @pl.when(me >= reaches[r])
            def _():
                pl.semaphore_signal(
                    ready.at[r], inc=1, device_id={"ctx": me - reaches[r]}, device_id_type=MESH)

            @pl.when(me + reaches[r] < devices)
            def _():
                pl.semaphore_signal(
                    ready.at[r], inc=1, device_id={"ctx": me + reaches[r]}, device_id_type=MESH)

    def hear(r):
        if r < len(reaches):
            pl.semaphore_wait(
                ready.at[r],
                (me >= reaches[r]).astype(jnp.int32)
                + (me + reaches[r] < devices).astype(jnp.int32))

    def cols(c):
        return pl.ds(c * wide, wide)

    def send_inc(c):
        return pltpu.make_async_remote_copy(
            handed_hbm.at[0, :, cols(c)], inc.at[:, cols(c)], inc_s.at[c], inc_r.at[c],
            device_id={"pipe": ahead}, device_id_type=MESH)

    def send_z(c):
        return pltpu.make_async_remote_copy(
            zz.at[pl.ds(0, count), cols(c)], zz.at[pl.ds(count, count), cols(c)],
            z_s.at[c], z_r.at[c],
            device_id={"ctx": lax.rem(me + 1, devices)}, device_id_type=MESH)

    def send_g(c):
        return pltpu.make_async_remote_copy(
            gg.at[pl.ds(0, count), cols(c)], gg.at[pl.ds(count, count), cols(c)],
            g_s.at[c], g_r.at[c],
            device_id={"ctx": lax.rem(me + devices - 1, devices)}, device_id_type=MESH)

    def send_rim(c):
        return pltpu.make_async_remote_copy(
            dsc.at[:, pl.ds(0, RIM), cols(c)], dsc.at[:, pl.ds(count, RIM), cols(c)],
            rim_s.at[c], rim_r.at[c],
            device_id={"ctx": lax.rem(me + devices - 1, devices)}, device_id_type=MESH)

    def send_part(o):
        return pltpu.make_async_remote_copy(
            part.at[o], parts_in.at[me], rs_s.at[o], rs_r.at[me],
            device_id={"ctx": low + o}, device_id_type=MESH)

    def take_part(peer):
        return pltpu.make_async_remote_copy(
            part.at[0], parts_in.at[peer], rs_s.at[0], rs_r.at[peer],
            device_id={"ctx": peer}, device_id_type=MESH)

    def send_sum(k):
        return pltpu.make_async_remote_copy(
            gath.at[me - low], gath.at[me - low], ag_s.at[k], ag_r.at[me - low],
            device_id={"ctx": lax.rem(me + k, devices)}, device_id_type=MESH)

    def take_sum(o):
        return pltpu.make_async_remote_copy(
            gath.at[o], gath.at[o], ag_s.at[0], ag_r.at[o],
            device_id={"ctx": low + o}, device_id_type=MESH)

    for c in range(chunks):
        send_inc(c).start()
    tell(0)

    loads[1].wait()
    loads[2].wait()
    for c in range(chunks):
        z = qkv[1, :, cols(c)].astype(F32) * qkv[2, :, cols(c)].astype(F32)
        zz[pl.ds(0, count), cols(c)] = z.astype(BF16)

        @pl.when(after)
        def _():
            send_z(c).start()

    @pl.when(first)
    def _():
        zz[pl.ds(count, count), :] = jnp.zeros((count, channels), BF16)

    @pl.when(last)
    def _():
        gg[pl.ds(count, count), :] = jnp.zeros((count, channels), BF16)
        dsc[:, pl.ds(count, RIM), :] = jnp.zeros((3, RIM, channels), F32)

    square = (count, count)
    down = lax.broadcasted_iota(jnp.int32, square, 0)
    across = lax.broadcasted_iota(jnp.int32, square, 1)
    base = me * count

    def one(flag):
        return jnp.where(flag, 1.0, 0.0).astype(F32)

    pos_down = positions(base + down[:, :LANES], docs_ref)
    lag = down - across
    m_own[...] = one((lag >= 0) & (lag <= pos_down)).astype(BF16)
    m_prev[...] = one((lag < 0) & (lag + count <= pos_down)).astype(BF16)
    turned = count - 1 - down
    pos_turned = positions(base + turned, docs_ref)
    lag = turned - across
    r_own[...] = one((lag >= 0) & (lag <= pos_turned))
    r_prev[...] = one((lag < 0) & (lag + count <= pos_turned))
    line = lax.broadcasted_iota(jnp.int32, (8, count), 1)
    pos_line = positions(base + line, docs_ref)[0:1]
    pos_ahead = positions(base + count + line, docs_ref)[0:1]
    lag = across - down
    t_own[...] = one((lag >= 0) & (lag <= pos_line)).astype(BF16)
    more = jnp.where(last, 0, 1)
    t_next[...] = one((lag < 0) & (lag + count <= pos_ahead) & (more > 0)).astype(BF16)
    for j in range(1, u_rows.shape[0] + 1):
        rows = base + down[:, :LANES] + j
        u_rows[j - 1] = one((j <= positions(rows, docs_ref)) & (rows < devices * count))
    lane_group = lax.broadcasted_iota(jnp.int32, (count, LANES), 1) // members
    for g in range(per_tile):
        lane_mask[g] = one(lane_group == g).astype(BF16)
    straight = one(down == across).astype(BF16)
    lapped = one((down + across == 0) | (down + across == count)).astype(BF16)
    flip = one(down + across == count - 1)
    sides = (((0,), (0,)), ((), ()))
    for copy in params:
        copy.wait()
    fdir[...] = lax.dot_general(filt[...], straight, sides, preferred_element_type=F32)
    frev[...] = lax.dot_general(filt[...], lapped, sides, preferred_element_type=F32)
    shortf[...] = short_in[...].astype(F32)

    def toeplitz(source, lhs, tile, near, far):
        for g in range(per_tile):
            row = tile * per_tile + g
            full = jnp.broadcast_to(source[row:row + 1, :], (STRIP, count))
            strip = pltpu.roll(full, 0, 1, stride=1, stride_axis=0).astype(BF16)
            for a in range(count // STRIP):
                ring = pltpu.roll(strip, a * STRIP, 1) if a else strip
                rows = slice(a * STRIP, (a + 1) * STRIP)
                at = slice(g * count + a * STRIP, g * count + (a + 1) * STRIP)
                lhs[tile, at, :count] = ring * near[rows]
                lhs[tile, at, count:] = ring * far[rows]

    def picked(product):
        total = product[:count]
        for g in range(1, per_tile):
            total = jnp.where(lane_group == g, product[g * count:(g + 1) * count], total)
        return total

    def lanes(tile):
        return pl.ds(tile * LANES, LANES)

    def span(c):
        return range(c * tiles, (c + 1) * tiles)

    for tile in span(0):
        toeplitz(frev, lhs_f, tile, m_own, m_prev)

    for c in range(chunks):
        @pl.when(before)
        def _():
            send_z(c).wait_recv()

        for tile in span(c):
            product = jnp.dot(lhs_f[tile], zz[:, lanes(tile)], preferred_element_type=F32)
            ysc[:, lanes(tile)] = picked(product)
            if c + 1 < chunks:
                toeplitz(frev, lhs_f, tile + tiles, m_own, m_prev)
            toeplitz(fdir, lhs_b, tile, t_own, t_next)
        hear(c)
        tell(c + 1)
    for r in range(chunks, len(reaches)):
        hear(r)
        tell(r + 1)

    def backward(c):
        @pl.when(after)
        def _():
            send_g(c).wait_recv()

        for tile in span(c):
            product = jnp.dot(lhs_b[tile], gg[:, lanes(tile)], preferred_element_type=F32)
            mixed = picked(product)
            key = qkv[1, :, lanes(tile)].astype(F32)
            value = qkv[2, :, lanes(tile)].astype(F32)
            dsc[1, pl.ds(0, count), lanes(tile)] = (mixed * value).astype(BF16).astype(F32)
            dsc[2, pl.ds(0, count), lanes(tile)] = (mixed * key).astype(BF16).astype(F32)

        @pl.when(before)
        def _():
            send_rim(c).start()

    def store(c):
        return pltpu.make_async_copy(
            obuf.at[:, :, cols(c)], out_hbm.at[0, :, :, cols(c)], out_sem.at[c])

    def short(c):
        @pl.when(after)
        def _():
            send_rim(c).wait_recv()

        def one_tile(i, carry):
            at = pl.ds(pl.multiple_of((c * tiles + i) * LANES, LANES), LANES)
            for s in range(3):
                total = dsc[s, pl.ds(0, count), at] * shortf[s, pl.ds(0, 1), at]
                for j in range(1, u_rows.shape[0] + 1):
                    moved = dsc[s, pl.ds(j, count), at]
                    weight = shortf[s, pl.ds(j, 1), at]
                    total = total + (moved * weight) * u_rows[j - 1]
                obuf[s, :, at] = total.astype(BF16)
            return carry

        lax.fori_loop(0, tiles, one_tile, 0)
        store(c).start()

    loads[0].wait()
    for c in range(chunks):
        send_inc(c).wait_recv()
        wide_inc = inc[:, cols(c)].astype(F32)
        own = (wide_inc * qkv[0, :, cols(c)].astype(F32)).astype(BF16)
        gg[pl.ds(0, count), cols(c)] = own

        @pl.when(before)
        def _():
            send_g(c).start()

        dsc[0, pl.ds(0, count), cols(c)] = (wide_inc * ysc[:, cols(c)]).astype(BF16).astype(F32)
        gback[:, cols(c)] = jnp.dot(
            flip.astype(BF16), own, preferred_element_type=F32).astype(BF16)
        for i, tile in enumerate(span(c)):
            back = gback[:, lanes(tile)]
            for g in range(per_tile):
                lhs_p[i, g * count:(g + 1) * count, :] = back * lane_mask[g]
            product = lax.dot_general(
                lhs_p[i], zz[:, lanes(tile)], (((1,), (1,)), ((), ())),
                preferred_element_type=F32)
            sums = []
            for g in range(per_tile):
                near = product[g * count:(g + 1) * count, :count]
                far = product[g * count:(g + 1) * count, count:]
                both = near * r_own[...] + far * r_prev[...]
                slid = pltpu.roll(both, 0, 1, stride=1, stride_axis=0)
                sums.append(jnp.sum(slid, axis=0, keepdims=True))
            acc[pl.ds(tile * per_tile, per_tile), :] = jnp.concatenate(sums, axis=0)

        if c == chunks - 1:
            for o in range(owners):
                part[o] = acc[o * share:(o + 1) * share, :]

            def start_part(o, carry):
                @pl.when(me != low + o)
                def _():
                    send_part(o).start()
                return carry

            lax.fori_loop(0, owners, start_part, 0)
        if c >= 1:
            backward(c - 1)
        if c >= 2:
            short(c - 2)

    backward(chunks - 1)
    owner = (me >= low) & (me < low + owners)

    @pl.when(owner)
    def _():
        def land_part(k, total):
            peer = lax.rem(me + k, devices)
            take_part(peer).wait_recv()
            return total + parts_in[peer]

        gath[me - low] = lax.fori_loop(1, devices, land_part, part[me - low])

        def start_sum(k, carry):
            send_sum(k).start()
            return carry

        lax.fori_loop(1, devices, start_sum, 0)

    for c in range(max(chunks - 2, 0), chunks):
        short(c)

    def land_sum(o, carry):
        @pl.when(me != low + o)
        def _():
            take_sum(o).wait_recv()
        return carry

    lax.fori_loop(0, owners, land_sum, 0)
    for o in range(owners):
        acc[o * share:(o + 1) * share, :] = gath[o]
    summed = lax.dot_general(
        flip, acc[...], (((1,), (1,)), ((), ())),
        preferred_element_type=F32, precision=lax.Precision.HIGHEST)
    fg[...] = summed / math.sqrt(count * devices * members)
    put = pltpu.make_async_copy(fg, sum_hbm.at[0], sum_sem)
    put.start()

    def left(o, carry):
        @pl.when(me != low + o)
        def _():
            send_part(o).wait_send()
        return carry

    lax.fori_loop(0, owners, left, 0)

    @pl.when(owner)
    def _():
        def left_sum(k, carry):
            send_sum(k).wait_send()
            return carry

        lax.fori_loop(1, devices, left_sum, 0)

    for c in range(chunks):
        send_inc(c).wait_send()
        store(c).wait()

        @pl.when(after)
        def _():
            send_z(c).wait_send()

        @pl.when(before)
        def _():
            send_g(c).wait_send()
            send_rim(c).wait_send()

    put.wait()


def put_out(grad_in, sums_in, grad_out, sums_out, sems):
    copies = [
        pltpu.make_async_copy(grad_in.at[0, i], grad_out.at[0, i], sems.at[i])
        for i in range(grad_in.shape[1])
    ]
    copies.append(pltpu.make_async_copy(sums_in, sums_out, sems.at[grad_in.shape[1]]))
    for copy in copies:
        copy.start()
    for copy in copies:
        copy.wait()


def body(sections, devices, saved_qkv, handed, long_filter, short_filter, doc_lengths):
    _, _, count, channels = saved_qkv.shape
    _, taps, groups = long_filter.shape
    short_taps = short_filter.shape[2]
    owners = max(1, devices // 2)
    assert taps == count and groups % owners == 0
    chunks = max(1, math.gcd(channels // LANES, 4))
    tiles = channels // LANES // chunks
    per_tile = LANES // (channels // groups)
    share = groups // owners
    dma = pltpu.SemaphoreType.DMA
    vmem = pltpu.VMEM
    hbm = pl.BlockSpec(memory_space=pl.ANY)
    saved_qkv, handed, long_filter, short_filter = [
        pltpu.with_memory_space_constraint(x, pltpu.HBM)
        for x in (saved_qkv, handed, long_filter, short_filter)
    ]
    grads, sums = pl.pallas_call(
        functools.partial(kernel, sections, devices, chunks, owners),
        out_shape=(
            pltpu.VMEM(saved_qkv.shape, BF16),
            pltpu.VMEM(long_filter.shape, F32),
        ),
        in_specs=[pl.BlockSpec(memory_space=pltpu.SMEM), hbm, hbm, hbm, hbm],
        out_specs=(hbm, hbm),
        scratch_shapes=[
            vmem((3, count, channels), BF16),
            vmem((count, channels), BF16),
            vmem((2 * count, channels), BF16),
            vmem((2 * count, channels), BF16),
            vmem((count, channels), BF16),
            vmem((count, channels), F32),
            vmem((3, count + RIM, channels), F32),
            vmem((3, count, channels), BF16),
            vmem((chunks * tiles, per_tile * count, 2 * count), BF16),
            vmem((chunks * tiles, per_tile * count, 2 * count), BF16),
            vmem((tiles, per_tile * count, LANES), BF16),
            vmem((groups, count), F32),
            vmem((groups, count), F32),
            vmem((count, groups), BF16),
            vmem((3, short_taps, channels), BF16),
            vmem((3, short_taps, channels), F32),
            vmem((count, count), BF16),
            vmem((count, count), BF16),
            vmem((count, count), BF16),
            vmem((count, count), BF16),
            vmem((count, count), F32),
            vmem((count, count), F32),
            vmem((short_taps - 1, count, LANES), F32),
            vmem((per_tile, count, LANES), BF16),
            vmem((groups, count), F32),
            vmem((owners, share, count), F32),
            vmem((devices, share, count), F32),
            vmem((owners, share, count), F32),
            vmem((count, groups), F32),
            dma((3,)), dma((2,)), dma((chunks,)), dma(()),
            dma((chunks,)), dma((chunks,)),
            dma((chunks,)), dma((chunks,)),
            dma((chunks,)), dma((chunks,)),
            dma((chunks,)), dma((chunks,)),
            dma((owners,)), dma((devices,)),
            dma((devices,)), dma((owners,)),
            pltpu.SemaphoreType.REGULAR((max(1, devices.bit_length()),)),
        ],
        compiler_params=pltpu.CompilerParams(
            collective_id=0, has_side_effects=True, vmem_limit_bytes=56 * 1024 * 1024),
    )(doc_lengths, saved_qkv, handed, long_filter, short_filter)
    return pl.pallas_call(
        put_out,
        out_shape=(
            jax.ShapeDtypeStruct(saved_qkv.shape, BF16),
            jax.ShapeDtypeStruct(long_filter.shape, F32),
        ),
        in_specs=[hbm, hbm],
        out_specs=(hbm, hbm),
        scratch_shapes=[dma((saved_qkv.shape[1] + 1,))],
        compiler_params=pltpu.CompilerParams(vmem_limit_bytes=1024 * 1024),
    )(grads, sums)


def solution(mesh):
    return jax.shard_map(
        functools.partial(body, mesh.shape["pipe"], mesh.shape["ctx"]),
        mesh=mesh,
        in_specs=(
            P("pipe", None, "ctx", None),
            P("pipe", "ctx", None),
            P("pipe", None, None),
            P("pipe", None, None, None),
            P(),
        ),
        out_specs=(P("pipe", None, "ctx", None), P("pipe", None, None)),
        check_vma=False,
    )
```

time: 40.5 us -> 36.6 us (0.904)
  local copies, waits for them, and re-layouts: 3.39 us -> 0 us
    unnamed x4 -> x0, local copies, waits for them, and re-layouts: 3.39 us -> none
    pallas_call x1 -> x2, Pallas kernels: 35.9 us -> 35.6 us  [the longest x1 34.5 us: body(): pl.pallas_call(functools.partial(kernel, sections, devices, chunks, owner...]
where the time goes in v1:
time: 36.6 us; the launch traced here: 36.4 us
  Pallas kernels  35.6 us (97%)
  between operations  0.8 us (2%)
    pallas_call x1, Pallas kernels, body(): pl.pallas_call(functools.partial(kernel, sections, devices, chunks, owner...  34.5 us
    pallas_call x1, Pallas kernels, body(): pl.pallas_call(put_out, out_shape=(jax.ShapeDtypeStruct(saved_qkv.shape,...  1.18 us

profile of v1, /device:TPU:0, one launch (start us, length us, event | category | flops | bytes accessed | tf_op | source)
XLA Modules:
  0.0 36.4 jit_solution(8392828714264830878)
XLA Ops:
  0.6 34.5 %shard_map.68 = (bf16[1,3,128,2048]{3,2,1,0:T(8,128)(2,1)S(1)}, f32[1,128,128]{2,1,0:T(8,128)S(1)}) custom-call(s32[16]{0:T(128)} %docs_ref.1, bf16[1,3,128,2048]{3,2,1,0:T(8,128)(2,1)} %qkv_hbm.1, bf16[1,128,2048]{2,1,0:T(8,128)(2,1)} %handed_hbm.1, bf16[1,128,128]{2,1,0:T(8,128)(2,1)} %filt_hbm.1, bf16[1,3,3,2048]{3,2,1,0:T(4,128)(2,1)} %short_hbm.1), custom_call_target="tpu_custom_call" | custom-call | tf_op jit(solution)/shard_map/pallas_call | solution.py:438
  35.1 1.2 %shard_map.69 = (bf16[1,3,128,2048]{3,2,1,0:T(8,128)(2,1)}, f32[1,128,128]{2,1,0:T(8,128)}) custom-call(bf16[1,3,128,2048]{3,2,1,0:T(8,128)(2,1)S(1)} %get-tuple-element.4.grad_in, f32[1,128,128]{2,1,0:T(8,128)S(1)} %get-tuple-element.5.sums_in), custom_call_target="tpu_custom_call" | custom-call | tf_op jit(solution)/shard_map/pallas_call | solution.py:488

commit v2 on v1

--- a/solution.py
+++ b/solution.py
@@ -29,9 +29,9 @@
     sections, devices, chunks, owners,
     docs_ref, qkv_hbm, handed_hbm, filt_hbm, short_hbm,
     out_hbm, sum_hbm,
-    qkv, inc, zz, gg, gback, ysc, dsc, obuf, lhs_f, lhs_b, lhs_p, fdir, frev, filt, short_in, shortf,
+    qkv, inc, zz, gg, gback, ysc, dsc, obuf, fdir, frev, filt, short_in, shortf,
     m_own, m_prev, t_own, t_next, r_own, r_prev, u_rows, lane_mask,
-    acc, part, parts_in, gath, fg,
+    acc, part_a, part_b, parts_in_a, parts_in_b, gath_a, gath_b, fg,
     in_sem, par_sem, out_sem, sum_sem, inc_s, inc_r, z_s, z_r, g_s, g_r, rim_s, rim_r, rs_s, rs_r, ag_s, ag_r,
     ready,
 ):
@@ -43,7 +43,7 @@
     per_tile = LANES // members
     wide = channels // chunks
     tiles = wide // LANES
-    share = groups // owners
+    part, parts_in, gath = (part_a, part_b), (parts_in_a, parts_in_b), (gath_a, gath_b)
     low = (devices - owners) // 2
     first, last = me == 0, me == devices - 1
     ahead = lax.rem(sec + sections - 1, sections)
@@ -79,27 +79,30 @@
     while 2 ** len(reaches) < devices:
         reaches.append(2 ** len(reaches))
 
+    def reach(r):
+        return lax.shift_left(jnp.int32(1), jnp.int32(r))
+
     def tell(r):
-        if r < len(reaches):
-            @pl.when(me >= reaches[r])
-            def _():
-                pl.semaphore_signal(
-                    ready.at[r], inc=1, device_id={"ctx": me - reaches[r]}, device_id_type=MESH)
-
-            @pl.when(me + reaches[r] < devices)
-            def _():
-                pl.semaphore_signal(
-                    ready.at[r], inc=1, device_id={"ctx": me + reaches[r]}, device_id_type=MESH)
+        @pl.when((r < len(reaches)) & (me >= reach(r)))
+        def _():
+            pl.semaphore_signal(
+                ready.at[r], inc=1, device_id={"ctx": me - reach(r)}, device_id_type=MESH)
+
+        @pl.when((r < len(reaches)) & (me + reach(r) < devices))
+        def _():
+            pl.semaphore_signal(
+                ready.at[r], inc=1, device_id={"ctx": me + reach(r)}, device_id_type=MESH)
 
     def hear(r):
-        if r < len(reaches):
+        @pl.when(r < len(reaches))
+        def _():
             pl.semaphore_wait(
                 ready.at[r],
-                (me >= reaches[r]).astype(jnp.int32)
-                + (me + reaches[r] < devices).astype(jnp.int32))
+                (me >= reach(r)).astype(jnp.int32)
+                + (me + reach(r) < devices).astype(jnp.int32))
 
     def cols(c):
-        return pl.ds(c * wide, wide)
+        return pl.ds(pl.multiple_of(c * wide, wide), wide)
 
     def send_inc(c):
         return pltpu.make_async_remote_copy(
@@ -124,24 +127,24 @@
             rim_s.at[c], rim_r.at[c],
             device_id={"ctx": lax.rem(me + devices - 1, devices)}, device_id_type=MESH)
 
-    def send_part(o):
-        return pltpu.make_async_remote_copy(
-            part.at[o], parts_in.at[me], rs_s.at[o], rs_r.at[me],
+    def send_part(b, o):
+        return pltpu.make_async_remote_copy(
+            part[b].at[o], parts_in[b].at[me], rs_s.at[b, o], rs_r.at[b, me],
             device_id={"ctx": low + o}, device_id_type=MESH)
 
-    def take_part(peer):
-        return pltpu.make_async_remote_copy(
-            part.at[0], parts_in.at[peer], rs_s.at[0], rs_r.at[peer],
+    def take_part(b, peer):
+        return pltpu.make_async_remote_copy(
+            part[b].at[0], parts_in[b].at[peer], rs_s.at[b, 0], rs_r.at[b, peer],
             device_id={"ctx": peer}, device_id_type=MESH)
 
-    def send_sum(k):
-        return pltpu.make_async_remote_copy(
-            gath.at[me - low], gath.at[me - low], ag_s.at[k], ag_r.at[me - low],
+    def send_sum(b, k):
+        return pltpu.make_async_remote_copy(
+            gath[b].at[me - low], gath[b].at[me - low], ag_s.at[b, k], ag_r.at[b, me - low],
             device_id={"ctx": lax.rem(me + k, devices)}, device_id_type=MESH)
 
-    def take_sum(o):
-        return pltpu.make_async_remote_copy(
-            gath.at[o], gath.at[o], ag_s.at[0], ag_r.at[o],
+    def take_sum(b, o):
+        return pltpu.make_async_remote_copy(
+            gath[b].at[o], gath[b].at[o], ag_s.at[b, 0], ag_r.at[b, o],
             device_id={"ctx": low + o}, device_id_type=MESH)
 
     for c in range(chunks):
@@ -175,16 +178,21 @@
     def one(flag):
         return jnp.where(flag, 1.0, 0.0).astype(F32)
 
-    pos_down = positions(base + down[:, :LANES], docs_ref)
+    line = lax.broadcasted_iota(jnp.int32, (8, count), 1)
+
+    def upright(rows):
+        spread = jnp.broadcast_to(positions(rows, docs_ref)[0:1].astype(F32), square)
+        return spread.T.astype(jnp.int32)
+
+    pos_down = upright(base + line)
     lag = down - across
     m_own[...] = one((lag >= 0) & (lag <= pos_down)).astype(BF16)
     m_prev[...] = one((lag < 0) & (lag + count <= pos_down)).astype(BF16)
     turned = count - 1 - down
-    pos_turned = positions(base + turned, docs_ref)
+    pos_turned = upright(base + count - 1 - line)
     lag = turned - across
     r_own[...] = one((lag >= 0) & (lag <= pos_turned))
     r_prev[...] = one((lag < 0) & (lag + count <= pos_turned))
-    line = lax.broadcasted_iota(jnp.int32, (8, count), 1)
     pos_line = positions(base + line, docs_ref)[0:1]
     pos_ahead = positions(base + count + line, docs_ref)[0:1]
     lag = across - down
@@ -192,8 +200,8 @@
     more = jnp.where(last, 0, 1)
     t_next[...] = one((lag < 0) & (lag + count <= pos_ahead) & (more > 0)).astype(BF16)
     for j in range(1, u_rows.shape[0] + 1):
-        rows = base + down[:, :LANES] + j
-        u_rows[j - 1] = one((j <= positions(rows, docs_ref)) & (rows < devices * count))
+        rows = base + down + j
+        u_rows[j - 1] = one((j <= upright(base + line + j)) & (rows < devices * count))
     lane_group = lax.broadcasted_iota(jnp.int32, (count, LANES), 1) // members
     for g in range(per_tile):
         lane_mask[g] = one(lane_group == g).astype(BF16)
@@ -207,46 +215,39 @@
     frev[...] = lax.dot_general(filt[...], lapped, sides, preferred_element_type=F32)
     shortf[...] = short_in[...].astype(F32)
 
-    def toeplitz(source, lhs, tile, near, far):
+    def applied(filters, near, far, tile, source):
+        block = filters[pl.ds(pl.multiple_of(tile * per_tile, per_tile), per_tile), :]
+        strips = []
         for g in range(per_tile):
-            row = tile * per_tile + g
-            full = jnp.broadcast_to(source[row:row + 1, :], (STRIP, count))
+            full = jnp.broadcast_to(block[g:g + 1], (STRIP, count))
             strip = pltpu.roll(full, 0, 1, stride=1, stride_axis=0).astype(BF16)
             for a in range(count // STRIP):
                 ring = pltpu.roll(strip, a * STRIP, 1) if a else strip
                 rows = slice(a * STRIP, (a + 1) * STRIP)
-                at = slice(g * count + a * STRIP, g * count + (a + 1) * STRIP)
-                lhs[tile, at, :count] = ring * near[rows]
-                lhs[tile, at, count:] = ring * far[rows]
-
-    def picked(product):
+                strips.append(jnp.concatenate([ring * near[rows], ring * far[rows]], axis=1))
+        product = jnp.dot(
+            jnp.concatenate(strips, axis=0), source[:, lanes(tile)], preferred_element_type=F32)
         total = product[:count]
         for g in range(1, per_tile):
             total = jnp.where(lane_group == g, product[g * count:(g + 1) * count], total)
         return total
 
     def lanes(tile):
-        return pl.ds(tile * LANES, LANES)
-
-    def span(c):
-        return range(c * tiles, (c + 1) * tiles)
-
-    for tile in span(0):
-        toeplitz(frev, lhs_f, tile, m_own, m_prev)
-
-    for c in range(chunks):
+        return pl.ds(pl.multiple_of(tile * LANES, LANES), LANES)
+
+    def forward(c, carry):
         @pl.when(before)
         def _():
             send_z(c).wait_recv()
 
-        for tile in span(c):
-            product = jnp.dot(lhs_f[tile], zz[:, lanes(tile)], preferred_element_type=F32)
-            ysc[:, lanes(tile)] = picked(product)
-            if c + 1 < chunks:
-                toeplitz(frev, lhs_f, tile + tiles, m_own, m_prev)
-            toeplitz(fdir, lhs_b, tile, t_own, t_next)
+        for i in range(tiles):
+            tile = c * tiles + i
+            ysc[:, lanes(tile)] = applied(frev, m_own, m_prev, tile, zz)
         hear(c)
         tell(c + 1)
+        return carry
+
+    lax.fori_loop(0, chunks, forward, 0)
     for r in range(chunks, len(reaches)):
         hear(r)
         tell(r + 1)
@@ -256,9 +257,9 @@
         def _():
             send_g(c).wait_recv()
 
-        for tile in span(c):
-            product = jnp.dot(lhs_b[tile], gg[:, lanes(tile)], preferred_element_type=F32)
-            mixed = picked(product)
+        for i in range(tiles):
+            tile = c * tiles + i
+            mixed = applied(fdir, t_own, t_next, tile, gg)
             key = qkv[1, :, lanes(tile)].astype(F32)
             value = qkv[2, :, lanes(tile)].astype(F32)
             dsc[1, pl.ds(0, count), lanes(tile)] = (mixed * value).astype(BF16).astype(F32)
@@ -291,8 +292,7 @@
         lax.fori_loop(0, tiles, one_tile, 0)
         store(c).start()
 
-    loads[0].wait()
-    for c in range(chunks):
+    def pairs(c):
         send_inc(c).wait_recv()
         wide_inc = inc[:, cols(c)].astype(F32)
         own = (wide_inc * qkv[0, :, cols(c)].astype(F32)).astype(BF16)
@@ -303,14 +303,14 @@
             send_g(c).start()
 
         dsc[0, pl.ds(0, count), cols(c)] = (wide_inc * ysc[:, cols(c)]).astype(BF16).astype(F32)
-        gback[:, cols(c)] = jnp.dot(
+        gback[...] = jnp.dot(
             flip.astype(BF16), own, preferred_element_type=F32).astype(BF16)
-        for i, tile in enumerate(span(c)):
-            back = gback[:, lanes(tile)]
-            for g in range(per_tile):
-                lhs_p[i, g * count:(g + 1) * count, :] = back * lane_mask[g]
+        for i in range(tiles):
+            tile = c * tiles + i
+            back = gback[:, i * LANES:(i + 1) * LANES]
+            spread = jnp.concatenate([back * lane_mask[g] for g in range(per_tile)], axis=0)
             product = lax.dot_general(
-                lhs_p[i], zz[:, lanes(tile)], (((1,), (1,)), ((), ())),
+                spread, zz[:, lanes(tile)], (((1,), (1,)), ((), ())),
                 preferred_element_type=F32)
             sums = []
             for g in range(per_tile):
@@ -319,54 +319,85 @@
                 both = near * r_own[...] + far * r_prev[...]
                 slid = pltpu.roll(both, 0, 1, stride=1, stride_axis=0)
                 sums.append(jnp.sum(slid, axis=0, keepdims=True))
-            acc[pl.ds(tile * per_tile, per_tile), :] = jnp.concatenate(sums, axis=0)
-
-        if c == chunks - 1:
-            for o in range(owners):
-                part[o] = acc[o * share:(o + 1) * share, :]
-
-            def start_part(o, carry):
-                @pl.when(me != low + o)
-                def _():
-                    send_part(o).start()
-                return carry
-
-            lax.fori_loop(0, owners, start_part, 0)
-        if c >= 1:
-            backward(c - 1)
-        if c >= 2:
-            short(c - 2)
-
-    backward(chunks - 1)
+            acc[pl.ds(pl.multiple_of(tile * per_tile, per_tile), per_tile), :] = (
+                jnp.concatenate(sums, axis=0))
+
     owner = (me >= low) & (me < low + owners)
-
-    @pl.when(owner)
-    def _():
+    head = (chunks - 1) * (groups // chunks)
+    batches = [(b, begin, part[b].shape[1]) for b, begin in ((0, 0), (1, head))]
+
+    def scatter(b):
+        _, begin, share = batches[b]
+        for o in range(owners):
+            part[b][o] = acc[begin + o * share:begin + (o + 1) * share, :]
+
+        def start_part(o, carry):
+            @pl.when(me != low + o)
+            def _():
+                send_part(b, o).start()
+            return carry
+
+        lax.fori_loop(0, owners, start_part, 0)
+
+    def collect(b):
         def land_part(k, total):
             peer = lax.rem(me + k, devices)
-            take_part(peer).wait_recv()
-            return total + parts_in[peer]
-
-        gath[me - low] = lax.fori_loop(1, devices, land_part, part[me - low])
+            take_part(b, peer).wait_recv()
+            return total + parts_in[b][peer]
+
+        gath[b][me - low] = lax.fori_loop(1, devices, land_part, part[b][me - low])
 
         def start_sum(k, carry):
-            send_sum(k).start()
+            send_sum(b, k).start()
             return carry
 
         lax.fori_loop(1, devices, start_sum, 0)
 
-    for c in range(max(chunks - 2, 0), chunks):
-        short(c)
-
-    def land_sum(o, carry):
-        @pl.when(me != low + o)
-        def _():
-            take_sum(o).wait_recv()
+    loads[0].wait()
+
+    def step(c, carry):
+        @pl.when(c < chunks)
+        def _():
+            pairs(c)
+
+        @pl.when(c == chunks - 2)
+        def _():
+            scatter(0)
+
+        @pl.when(c == chunks - 1)
+        def _():
+            scatter(1)
+
+        @pl.when((c >= 1) & (c <= chunks))
+        def _():
+            backward(c - 1)
+
+        @pl.when((c == chunks - 1) & owner)
+        def _():
+            collect(0)
+
+        @pl.when((c == chunks) & owner)
+        def _():
+            collect(1)
+
+        @pl.when(c >= 2)
+        def _():
+            short(c - 2)
+
         return carry
 
-    lax.fori_loop(0, owners, land_sum, 0)
-    for o in range(owners):
-        acc[o * share:(o + 1) * share, :] = gath[o]
+    lax.fori_loop(0, chunks + 2, step, 0)
+
+    for b, begin, share in batches:
+        def land_sum(o, carry):
+            @pl.when(me != low + o)
+            def _():
+                take_sum(b, o).wait_recv()
+            return carry
+
+        lax.fori_loop(0, owners, land_sum, 0)
+        for o in range(owners):
+            acc[begin + o * share:begin + (o + 1) * share, :] = gath[b][o]
     summed = lax.dot_general(
         flip, acc[...], (((1,), (1,)), ((), ())),
         preferred_element_type=F32, precision=lax.Precision.HIGHEST)
@@ -374,21 +405,22 @@
     put = pltpu.make_async_copy(fg, sum_hbm.at[0], sum_sem)
     put.start()
 
-    def left(o, carry):
-        @pl.when(me != low + o)
-        def _():
-            send_part(o).wait_send()
-        return carry
-
-    lax.fori_loop(0, owners, left, 0)
-
-    @pl.when(owner)
-    def _():
-        def left_sum(k, carry):
-            send_sum(k).wait_send()
+    for b in range(2):
+        def left(o, carry):
+            @pl.when(me != low + o)
+            def _():
+                send_part(b, o).wait_send()
             return carry
 
-        lax.fori_loop(1, devices, left_sum, 0)
+        lax.fori_loop(0, owners, left, 0)
+
+        @pl.when(owner)
+        def _():
+            def left_sum(k, carry):
+                send_sum(b, k).wait_send()
+                return carry
+
+            lax.fori_loop(1, devices, left_sum, 0)
 
     for c in range(chunks):
         send_inc(c).wait_send()
@@ -423,11 +455,11 @@
     _, taps, groups = long_filter.shape
     short_taps = short_filter.shape[2]
     owners = max(1, devices // 2)
-    assert taps == count and groups % owners == 0
     chunks = max(1, math.gcd(channels // LANES, 4))
     tiles = channels // LANES // chunks
     per_tile = LANES // (channels // groups)
-    share = groups // owners
+    assert taps == count and chunks > 1 and groups % (owners * chunks) == 0
+    shares = [rest * (groups // (owners * chunks)) for rest in (chunks - 1, 1)]
     dma = pltpu.SemaphoreType.DMA
     vmem = pltpu.VMEM
     hbm = pl.BlockSpec(memory_space=pl.ANY)
@@ -448,13 +480,10 @@
             vmem((count, channels), BF16),
             vmem((2 * count, channels), BF16),
             vmem((2 * count, channels), BF16),
-            vmem((count, channels), BF16),
+            vmem((count, channels // chunks), BF16),
             vmem((count, channels), F32),
             vmem((3, count + RIM, channels), F32),
             vmem((3, count, channels), BF16),
-            vmem((chunks * tiles, per_tile * count, 2 * count), BF16),
-            vmem((chunks * tiles, per_tile * count, 2 * count), BF16),
-            vmem((tiles, per_tile * count, LANES), BF16),
             vmem((groups, count), F32),
             vmem((groups, count), F32),
             vmem((count, groups), BF16),
@@ -469,17 +498,17 @@
             vmem((short_taps - 1, count, LANES), F32),
             vmem((per_tile, count, LANES), BF16),
             vmem((groups, count), F32),
-            vmem((owners, share, count), F32),
-            vmem((devices, share, count), F32),
-            vmem((owners, share, count), F32),
+            *[vmem((owners, share, count), F32) for share in shares],
+            *[vmem((devices, share, count), F32) for share in shares],
+            *[vmem((owners, share, count), F32) for share in shares],
             vmem((count, groups), F32),
             dma((3,)), dma((2,)), dma((chunks,)), dma(()),
             dma((chunks,)), dma((chunks,)),
             dma((chunks,)), dma((chunks,)),
             dma((chunks,)), dma((chunks,)),
             dma((chunks,)), dma((chunks,)),
-            dma((owners,)), dma((devices,)),
-            dma((devices,)), dma((owners,)),
+            dma((2, owners)), dma((2, devices)),
+            dma((2, devices)), dma((2, owners)),
             pltpu.SemaphoreType.REGULAR((max(1, devices.bit_length()),)),
         ],
         compiler_params=pltpu.CompilerParams(

time: 36.6 us -> 33.6 us (0.918)
  Pallas kernels: 35.6 us -> 32.8 us
    pallas_call x1, Pallas kernels: 34.5 us -> 31.6 us  [body(): pl.pallas_call(functools.partial(kernel, sections, devices, chunks, owner...]
where the time goes in v2:
time: 33.6 us; the launch traced here: 33.4 us
  Pallas kernels  32.8 us (98%)
  between operations  0.64 us (2%)
    pallas_call x1, Pallas kernels, body(): pl.pallas_call(functools.partial(kernel, sections, devices, chunks, owner...  31.6 us
    pallas_call x1, Pallas kernels, body(): pl.pallas_call(put_out, out_shape=(jax.ShapeDtypeStruct(saved_qkv.shape,...  1.18 us

profile of v2, /device:TPU:0, one launch (start us, length us, event | category | flops | bytes accessed | tf_op | source)
XLA Modules:
  0.0 33.4 jit_solution(11768833995577259712)
XLA Ops:
  0.6 31.6 %shard_map.68 = (bf16[1,3,128,2048]{3,2,1,0:T(8,128)(2,1)S(1)}, f32[1,128,128]{2,1,0:T(8,128)S(1)}) custom-call(s32[16]{0:T(128)} %docs_ref.1, bf16[1,3,128,2048]{3,2,1,0:T(8,128)(2,1)} %qkv_hbm.1, bf16[1,128,2048]{2,1,0:T(8,128)(2,1)} %handed_hbm.1, bf16[1,128,128]{2,1,0:T(8,128)(2,1)} %filt_hbm.1, bf16[1,3,3,2048]{3,2,1,0:T(4,128)(2,1)} %short_hbm.1), custom_call_target="tpu_custom_call" | custom-call | tf_op jit(solution)/shard_map/pallas_call | solution.py:470
  32.2 1.2 %shard_map.69 = (bf16[1,3,128,2048]{3,2,1,0:T(8,128)(2,1)}, f32[1,128,128]{2,1,0:T(8,128)}) custom-call(bf16[1,3,128,2048]{3,2,1,0:T(8,128)(2,1)S(1)} %get-tuple-element.4.grad_in, f32[1,128,128]{2,1,0:T(8,128)S(1)} %get-tuple-element.5.sums_in), custom_call_target="tpu_custom_call" | custom-call | tf_op jit(solution)/shard_map/pallas_call | solution.py:517

commit v3 on v2

--- a/solution.py
+++ b/solution.py
@@ -29,7 +29,7 @@
     sections, devices, chunks, owners,
     docs_ref, qkv_hbm, handed_hbm, filt_hbm, short_hbm,
     out_hbm, sum_hbm,
-    qkv, inc, zz, gg, gback, ysc, dsc, obuf, fdir, frev, filt, short_in, shortf,
+    qkv, inc, zz, gg, gback, dsc, obuf, fdir, frev, filt, short_in, shortf,
     m_own, m_prev, t_own, t_next, r_own, r_prev, u_rows, lane_mask,
     acc, part_a, part_b, parts_in_a, parts_in_b, gath_a, gath_b, fg,
     in_sem, par_sem, out_sem, sum_sem, inc_s, inc_r, z_s, z_r, g_s, g_r, rim_s, rim_r, rs_s, rs_r, ag_s, ag_r,
@@ -160,6 +160,9 @@
         @pl.when(after)
         def _():
             send_z(c).start()
+
+    hear(0)
+    tell(1)
 
     @pl.when(first)
     def _():
@@ -215,6 +218,9 @@
     frev[...] = lax.dot_general(filt[...], lapped, sides, preferred_element_type=F32)
     shortf[...] = short_in[...].astype(F32)
 
+    hear(1)
+    tell(2)
+
     def applied(filters, near, far, tile, source):
         block = filters[pl.ds(pl.multiple_of(tile * per_tile, per_tile), per_tile), :]
         strips = []
@@ -235,22 +241,14 @@
     def lanes(tile):
         return pl.ds(pl.multiple_of(tile * LANES, LANES), LANES)
 
-    def forward(c, carry):
-        @pl.when(before)
-        def _():
-            send_z(c).wait_recv()
-
+    rounds = pl.cdiv(max(len(reaches) - 2, 1), chunks - 2)
+
+    def forward(c):
         for i in range(tiles):
-            tile = c * tiles + i
-            ysc[:, lanes(tile)] = applied(frev, m_own, m_prev, tile, zz)
-        hear(c)
-        tell(c + 1)
-        return carry
-
-    lax.fori_loop(0, chunks, forward, 0)
-    for r in range(chunks, len(reaches)):
-        hear(r)
-        tell(r + 1)
+            at = lanes(c * tiles + i)
+            total = applied(frev, m_own, m_prev, c * tiles + i, zz)
+            dsc[0, pl.ds(0, count), at] = (
+                inc[:, at].astype(F32) * total).astype(BF16).astype(F32)
 
     def backward(c):
         @pl.when(after)
@@ -302,7 +300,10 @@
         def _():
             send_g(c).start()
 
-        dsc[0, pl.ds(0, count), cols(c)] = (wide_inc * ysc[:, cols(c)]).astype(BF16).astype(F32)
+        @pl.when(before)
+        def _():
+            send_z(c).wait_recv()
+
         gback[...] = jnp.dot(
             flip.astype(BF16), own, preferred_element_type=F32).astype(BF16)
         for i in range(tiles):
@@ -368,6 +369,16 @@
         def _():
             scatter(1)
 
+        @pl.when(c < chunks)
+        def _():
+            forward(c)
+
+        @pl.when(c < chunks - 2)
+        def _():
+            for q in range(rounds):
+                hear(c * rounds + q + 2)
+                tell(c * rounds + q + 3)
+
         @pl.when((c >= 1) & (c <= chunks))
         def _():
             backward(c - 1)
@@ -458,7 +469,7 @@
     chunks = max(1, math.gcd(channels // LANES, 4))
     tiles = channels // LANES // chunks
     per_tile = LANES // (channels // groups)
-    assert taps == count and chunks > 1 and groups % (owners * chunks) == 0
+    assert taps == count and chunks > 2 and groups % (owners * chunks) == 0
     shares = [rest * (groups // (owners * chunks)) for rest in (chunks - 1, 1)]
     dma = pltpu.SemaphoreType.DMA
     vmem = pltpu.VMEM
@@ -481,7 +492,6 @@
             vmem((2 * count, channels), BF16),
             vmem((2 * count, channels), BF16),
             vmem((count, channels // chunks), BF16),
-            vmem((count, channels), F32),
             vmem((3, count + RIM, channels), F32),
             vmem((3, count, channels), BF16),
             vmem((groups, count), F32),

time: 33.6 us -> 32.5 us (0.967)
  Pallas kernels: 32.8 us -> 31.7 us
    pallas_call x1, Pallas kernels: 31.6 us -> 30.6 us  [body(): pl.pallas_call(functools.partial(kernel, sections, devices, chunks, owner...]
where the time goes in v3:
time: 32.5 us; the launch traced here: 32.4 us
  Pallas kernels  31.7 us (98%)
  between operations  0.64 us (2%)
    pallas_call x1, Pallas kernels, body(): pl.pallas_call(functools.partial(kernel, sections, devices, chunks, owner...  30.6 us
    pallas_call x1, Pallas kernels, body(): pl.pallas_call(put_out, out_shape=(jax.ShapeDtypeStruct(saved_qkv.shape,...  1.18 us

profile of v3, /device:TPU:0, one launch (start us, length us, event | category | flops | bytes accessed | tf_op | source)
XLA Modules:
  0.0 32.4 jit_solution(8732543523003962832)
XLA Ops:
  0.6 30.6 %shard_map.68 = (bf16[1,3,128,2048]{3,2,1,0:T(8,128)(2,1)S(1)}, f32[1,128,128]{2,1,0:T(8,128)S(1)}) custom-call(s32[16]{0:T(128)} %docs_ref.1, bf16[1,3,128,2048]{3,2,1,0:T(8,128)(2,1)} %qkv_hbm.1, bf16[1,128,2048]{2,1,0:T(8,128)(2,1)} %handed_hbm.1, bf16[1,128,128]{2,1,0:T(8,128)(2,1)} %filt_hbm.1, bf16[1,3,3,2048]{3,2,1,0:T(4,128)(2,1)} %short_hbm.1), custom_call_target="tpu_custom_call" | custom-call | tf_op jit(solution)/shard_map/pallas_call | solution.py:481
  31.2 1.2 %shard_map.69 = (bf16[1,3,128,2048]{3,2,1,0:T(8,128)(2,1)}, f32[1,128,128]{2,1,0:T(8,128)}) custom-call(bf16[1,3,128,2048]{3,2,1,0:T(8,128)(2,1)S(1)} %get-tuple-element.4.grad_in, f32[1,128,128]{2,1,0:T(8,128)S(1)} %get-tuple-element.5.sums_in), custom_call_target="tpu_custom_call" | custom-call | tf_op jit(solution)/shard_map/pallas_call | solution.py:527
